TPU v7x, 256 devices: a whole 4x4x8 slice. The times are simulated.
256 devices in a mesh: heads: 4 (over x), pages: 64 (over z, y, core).
Axes of the slice: x: 4, y: 4, z: 8, core: 2. Of those that a mesh axis runs over, the one named last changes fastest.
Arguments:
- queries: bfloat16 [4608, 16, 128], P('pages', 'heads'), may hold values from -60 to 60
- keys: bfloat16 [4608, 16, 128], P('pages', 'heads'), may hold values from -6 to 6
- values: bfloat16 [4608, 16, 128], P('pages', 'heads'), may hold values from -6 to 6
- key_cache: bfloat16 [768, 128, 16, 128], P('pages', None, 'heads'), may hold values from -6 to 6
- value_cache: bfloat16 [768, 128, 16, 128], P('pages', None, 'heads'), may hold values from -6 to 6
- cache_len: int32 [6], replicated, may hold values from 0 to 15616, as said below
- page_table: int32 [6, 122], replicated, may hold values from 0 to 767, as said below
- append_slots: int32 [6, 6], replicated, may hold values from 0 to 767
- out_weight: bfloat16 [2048, 4096], P('heads', 'pages'), may hold values from -0.125 to 0.125
- out_bias: float32 [4096], P('heads'), may hold values from -3 to 3
Outputs:
- hidden: bfloat16 [4608, 4096], P('pages', 'heads')
- key_cache_out: bfloat16 [768, 128, 16, 128], P('pages', None, 'heads')
- value_cache_out: bfloat16 [768, 128, 16, 128], P('pages', None, 'heads')
Inputs may be any that keep to these rules, and one draw needn't show every extreme that they name: Every entry of page_table and append_slots together is a different slot. `cache_len`: A multiple of 128; some request has exactly 15616.
All inputs are finite; a program needn't handle non-finite values.
Results may differ from a plain program's by a relative error of at most 0.018.
Values may be sent and summed in bfloat16 or wider, within the bound.
A program may use at most 128 MiB of HBM per device.

v0:
```python
import math
import jax
import jax.numpy as jnp
from jax import lax
from jax.sharding import PartitionSpec as P

ROT = 32
PAGE = 128
low_score = -1e30


def rotate(vectors, positions):
    half_rot = ROT // 2
    inv_freq = 10000.0 ** (-2.0 * jnp.arange(half_rot, dtype=jnp.float32) / ROT)
    angles = positions[:, None] * inv_freq[None, :]
    cosine = jnp.cos(angles)[:, None, :]
    sine = jnp.sin(angles)[:, None, :]
    first_half = vectors[..., :half_rot]
    second_half = vectors[..., half_rot:ROT]
    return jnp.concatenate(
        [
            first_half * cosine - second_half * sine,
            second_half * cosine + first_half * sine,
            vectors[..., ROT:],
        ],
        axis=-1,
    )


def per_device(
    queries,
    keys,
    values,
    key_cache,
    value_cache,
    cache_len,
    page_table,
    append_slots,
    out_weight,
    out_bias,
):
    tok_dev, head_count, head_dim = queries.shape
    requests = cache_len.shape[0]
    max_pages = page_table.shape[1]
    new_pages = append_slots.shape[1]
    span_len = new_pages * PAGE
    slot_count = key_cache.shape[0]
    device_at = lax.axis_index("pages")
    token_ids = device_at * tok_dev + jnp.arange(tok_dev, dtype=jnp.int32)
    request_ids = token_ids // span_len
    request_grid = jnp.arange(requests, dtype=jnp.int32)
    starts = jnp.sum(
        jnp.where(request_ids[:, None] == request_grid[None, :], cache_len[None, :], 0), axis=1
    )
    positions = (starts + token_ids % span_len).astype(jnp.float32)
    rotated_q = rotate(queries.astype(jnp.float32), positions).astype(jnp.bfloat16)
    rotated_k = rotate(keys.astype(jnp.float32), positions).astype(jnp.bfloat16)
    all_q, all_k, all_v = (
        lax.all_gather(rotated_q, "pages", axis=0, tiled=True),
        lax.all_gather(rotated_k, "pages", axis=0, tiled=True),
        lax.all_gather(values, "pages", axis=0, tiled=True),
    )
    my_slots = device_at * slot_count + jnp.arange(slot_count, dtype=jnp.int32)
    cached_hit = page_table.reshape(-1)[None, :] == my_slots[:, None]
    fresh_hit = append_slots.reshape(-1)[None, :] == my_slots[:, None]
    is_cached = jnp.any(cached_hit, axis=1)
    is_fresh = jnp.any(fresh_hit, axis=1)
    cached_index = jnp.sum(
        jnp.where(cached_hit, jnp.arange(requests * max_pages, dtype=jnp.int32)[None, :], 0), axis=1
    )
    fresh_index = jnp.sum(
        jnp.where(fresh_hit, jnp.arange(requests * new_pages, dtype=jnp.int32)[None, :], 0), axis=1
    )
    slot_request = jnp.where(is_fresh, fresh_index // new_pages, cached_index // max_pages)
    slot_page = jnp.where(is_fresh, fresh_index % new_pages, cached_index % max_pages)
    slot_length = jnp.sum(
        jnp.where(slot_request[:, None] == request_grid[None, :], cache_len[None, :], 0), axis=1
    )
    page_shape = (requests * new_pages, PAGE, head_count, head_dim)
    key_out = jnp.where(
        is_fresh[:, None, None, None],
        jnp.take(all_k.reshape(page_shape), fresh_index, axis=0),
        key_cache,
    )
    value_out = jnp.where(
        is_fresh[:, None, None, None],
        jnp.take(all_v.reshape(page_shape), fresh_index, axis=0),
        value_cache,
    )
    query_blocks = all_q.reshape(requests, span_len, head_count, head_dim)
    score_scale = 1.0 / math.sqrt(head_dim)
    query_offsets = jnp.arange(span_len, dtype=jnp.int32)
    key_offsets = jnp.arange(PAGE, dtype=jnp.int32)

    def slot_scores(slot):
        request = slot_request[slot]
        query_block = lax.dynamic_index_in_dim(query_blocks, request, 0, keepdims=False)
        key_block = lax.dynamic_index_in_dim(key_out, slot, 0, keepdims=False)
        scores = (
            jnp.einsum("qhd,khd->hqk", query_block, key_block, preferred_element_type=jnp.float32)
            * score_scale
        )
        length = slot_length[slot]
        base_pos = slot_page[slot] * PAGE + key_offsets
        cached_ok = is_cached[slot] & (base_pos < length)
        fresh_ok = is_fresh[slot] & (base_pos[None, :] <= query_offsets[:, None])
        allowed = cached_ok[None, :] | fresh_ok
        return (jnp.where(allowed[None], scores, low_score), request, allowed)

    def over_slots(step, start):
        return lax.fori_loop(0, slot_count, step, start)

    def peak_step(slot, peaks):
        scores, request, allowed = slot_scores(slot)
        local_max = jnp.transpose(jnp.max(scores, axis=2))
        earlier = lax.dynamic_index_in_dim(peaks, request, 0, keepdims=False)
        return lax.dynamic_update_index_in_dim(peaks, jnp.maximum(earlier, local_max), request, 0)

    peaks = over_slots(
        peak_step, jnp.full((requests, span_len, head_count), low_score, jnp.float32)
    )
    peaks = lax.pmax(peaks.astype(jnp.bfloat16), "pages").astype(peaks.dtype)

    def weigh_step(slot, carry):
        weighted, totals = carry
        scores, request, allowed = slot_scores(slot)
        row_peak = jnp.transpose(lax.dynamic_index_in_dim(peaks, request, 0, keepdims=False))
        weights = jnp.exp(scores - row_peak[:, :, None])
        value_block = lax.dynamic_index_in_dim(value_out, slot, 0, keepdims=False)
        contrib = jnp.einsum(
            "hqk,khd->qhd",
            weights.astype(jnp.bfloat16),
            value_block,
            preferred_element_type=jnp.float32,
        )
        earlier = lax.dynamic_index_in_dim(weighted, request, 0, keepdims=False)
        weighted = lax.dynamic_update_index_in_dim(weighted, earlier + contrib, request, 0)
        row_sums = jnp.transpose(jnp.sum(weights, axis=2))
        earlier_sums = lax.dynamic_index_in_dim(totals, request, 0, keepdims=False)
        totals = lax.dynamic_update_index_in_dim(totals, earlier_sums + row_sums, request, 0)
        return (weighted, totals)

    start_sums = (
        jnp.zeros((requests, span_len, head_count, head_dim), jnp.float32),
        jnp.zeros((requests, span_len, head_count), jnp.float32),
    )
    weighted, totals = over_slots(weigh_step, start_sums)
    weighted, totals = (
        lax.psum_scatter(
            weighted.reshape(requests * span_len, head_count * head_dim),
            "pages",
            scatter_dimension=0,
            tiled=True,
        ),
        lax.psum_scatter(
            totals.reshape(requests * span_len, head_count),
            "pages",
            scatter_dimension=0,
            tiled=True,
        ),
    )
    attended = (
        (weighted.reshape(tok_dev, head_count, head_dim) / totals[:, :, None])
        .reshape(tok_dev, head_count * head_dim)
        .astype(jnp.bfloat16)
    )
    projected = jnp.dot(
        attended,
        lax.all_gather(out_weight, "pages", axis=1, tiled=True),
        preferred_element_type=jnp.float32,
    )
    summed = lax.psum_scatter(
        projected.astype(jnp.bfloat16), "heads", scatter_dimension=1, tiled=True
    ).astype(jnp.float32)
    hidden = (summed + out_bias[None, :]).astype(jnp.bfloat16)
    return (hidden, key_out, value_out)


def solution(mesh):
    placed = (
        P("pages", "heads", None),
        P("pages", "heads", None),
        P("pages", "heads", None),
        P("pages", None, "heads", None),
        P("pages", None, "heads", None),
        P(),
        P(),
        P(),
        P("heads", "pages"),
        P("heads"),
    )
    return jax.shard_map(
        per_device,
        mesh=mesh,
        in_specs=placed,
        out_specs=(
            P("pages", "heads"),
            P("pages", None, "heads", None),
            P("pages", None, "heads", None),
        ),
        check_vma=False,
    )
```

profile of v0, /device:TPU:8, one launch (start us, length us, event | category | flops | bytes accessed | tf_op | source)
XLA Modules:
  0.0 1257.5 jit_solution(8616648984599023867)
XLA Ops:
  14.0 78.4 %all-gather.9.cloned.1.call-done = bf16[4608,4,128]{2,0,1:T(8,128)(2,1)} async-done(((bf16[72,4,128]{2,0,1:T(8,128)(2,1)}), bf16[4608,4,128]{2,0,1:T(8,128)(2,1)}) %all-gather.9.cloned.1.call-update) | async-done | bytes 4718608 | tf_op jit(solution)/shard_map/all_gather | solution.py:60
  92.4 6.3 copy.77
  98.7 73.7 %all-gather.5.cloned.1.call-done = bf16[4608,4,128]{2,0,1:T(8,128)(2,1)} async-done(((bf16[72,4,128]{2,0,1:T(8,128)(2,1)}), bf16[4608,4,128]{2,0,1:T(8,128)(2,1)}) %all-gather.5.cloned.1.call-update) | async-done | bytes 4718608 | tf_op jit(solution)/shard_map/all_gather | solution.py:61
  172.4 6.4 copy.71
  178.8 3.2 gather_fusion.1
  182.0 3.2 gather_fusion
  185.2 67.2 %all-gather.7.cloned.1.call-done = bf16[4608,4,128]{2,0,1:T(8,128)(2,1)} async-done(((bf16[72,4,128]{2,0,1:T(8,128)(2,1)}), bf16[4608,4,128]{2,0,1:T(8,128)(2,1)}) %all-gather.7.cloned.1.call-update) | async-done | bytes 4718608 | tf_op jit(solution)/shard_map/all_gather | solution.py:59
  252.5 5.2 copy.81
  260.0 109.8 %while.30 = (s32[]{:T(128)}, bf16[6,768,4]{1,2,0:T(4,128)(2,1)S(1)}, s32[12]{0:T(128)S(1)}, pred[12]{0:T(512)(128)(4,1)S(1)}, s32[12]{0:T(128)S(1)}, /*index=5*/...) while((s32[]{:T(128)}, ...), condition=%wide.region_8.10_spmd.clone, body=%wide.region_6.9_spmd.clone.sunk | while | flops 102147592 | bytes 1153013 | solution.py:111
  369.8 244.9 %pmax.7 = bf16[6,768,4]{1,2,0:T(4,128)(2,1)S(1)} all-reduce(bf16[6,768,4]{1,2,0:T(4,128)(2,1)S(1)} %get-tuple-element.418), channel_id=1, replica_groups=mesh['heads'=4,'pages'=64] {'pages'}, use_global_device_ids=true, to_apply=%region_9.11 | all-reduce | flops 18432 | bytes 73728 | tf_op jit(solution)/shard_map/pmax | solution.py:122
  614.7 4.8 broadcast_in_dim.197.clone
  619.5 196.1 %while.31 = (s32[]{:T(128)}, f32[6,768,4,128]{3,2,1,0:T(4,128)}, f32[6,768,4]{1,2,0:T(4,128)S(1)}, s32[12]{0:T(128)S(1)}, bf16[12,128,4,128]{3,1,2,0:T(8,128)(2,...) while((s32[]{:T(128)}, f32[6,768,4,128]{3,2,1,0:T(4,128)}, ...), condition=%wide.region_12.14_spmd.clone, body=%wide.region_10.13_spmd.clone.sunk | while | flops 203981312 | bytes 18659864 | solution.py:111
  627.3 2.6 fusion.53
  643.7 2.6 fusion.53
  660.0 2.6 fusion.53
  676.3 2.6 fusion.53
  692.6 2.6 fusion.53
  709.0 2.6 fusion.53
  725.3 2.6 fusion.53
  741.7 2.6 fusion.53
  758.0 2.6 fusion.53
  774.3 2.6 fusion.53
  790.7 2.6 fusion.53
  807.1 2.6 fusion.53
  816.9 8.4 copy.105
  827.3 158.9 %all-reduce.4.cloned.1.call-done = f32[4608,4]{0,1:T(4,128)} async-done(((f32[4608,4]{0,1:T(4,128)}), f32[4608,4]{0,1:T(4,128)}) %all-reduce.4.cloned.1.call-update) | async-done | bytes 73744
  987.0 77.0 %all-gather.11.cloned.1.call-done = bf16[512,4096]{0,1:T(8,128)(2,1)} async-done(((bf16[512,64]{0,1:T(8,128)(2,1)}), bf16[512,4096]{0,1:T(8,128)(2,1)}) %all-gather.11.cloned.1.call-update) | async-done | bytes 4194320 | tf_op jit(solution)/shard_map/all_gather | solution.py:169
  1064.1 156.9 %reduce-scatter.8.cloned.1.call-done = f32[72,512]{1,0:T(8,128)} async-done(((f32[4608,512]{1,0:T(8,128)}), f32[72,512]{1,0:T(8,128)}) %reduce-scatter.8.cloned.1.call-update) | async-done | bytes 147472
  1221.1 4.5 convolution_convert_fusion
  1225.6 3.9 copy.85
  1229.5 2.4 copy.86
  1231.9 17.2 %reduce-scatter.6.cloned.1.call-done = bf16[72,1024]{1,0:T(8,128)(2,1)} async-done(((bf16[72,4096]{1,0:T(8,128)(2,1)}), bf16[72,1024]{1,0:T(8,128)(2,1)}) %reduce-scatter.6.cloned.1.call-update) | async-done | bytes 147472 | tf_op jit(solution)/shard_map/reduce_scatter | solution.py:172
  (394 shorter events, 224.6 us)
Async XLA Ops:
  7.2 6.6 copy-start.9
  7.2 4.8 copy-start.4
  7.2 4.0 copy-start.5
  7.2 5.8 copy-start.7
  7.2 5.8 copy-start.8
  7.2 85.2 %all-gather.9.cloned.1.call-start = ((), (), s32[]{:S(2)}) async-start(), calls=%async_computation.4 | async-start | bytes 4792320 | tf_op jit(solution)/shard_map/all_gather | solution.py:60
  11.2 161.3 %all-gather.5.cloned.1.call-start = ((), (), s32[]{:S(2)}) async-start(), calls=%async_computation.2 | async-start | bytes 4792320 | tf_op jit(solution)/shard_map/all_gather | solution.py:61
  11.9 240.5 %all-gather.7.cloned.1.call-start = ((), (), s32[]{:S(2)}) async-start(), calls=%async_computation.3 | async-start | bytes 4792320 | tf_op jit(solution)/shard_map/all_gather | solution.py:59
  12.9 973.3 %all-reduce.4.cloned.1.call-start = ((), (), s32[]{:S(2)}) async-start(), calls=%async_computation.7 | async-start | bytes 147456
  252.5 5.2 copy-start.1
  252.5 5.2 copy-start.2
  815.6 0.6 copy-start.3
  816.3 247.8 %all-gather.11.cloned.1.call-start = ((), (), s32[]{:S(2)}) async-start(), calls=%async_computation.5 | async-start | bytes 4259840 | tf_op jit(solution)/shard_map/all_gather | solution.py:169
  816.9 404.0 %reduce-scatter.8.cloned.1.call-start = ((), (), s32[]{:S(2)}) async-start(), calls=%async_computation.8 | async-start | bytes 9584640
  825.4 0.7 copy-start.10
  825.4 423.6 %reduce-scatter.6.cloned.1.call-start = ((), (), s32[]{:S(2)}) async-start(), calls=%async_computation.6 | async-start | bytes 737280 | tf_op jit(solution)/shard_map/reduce_scatter | solution.py:172
  1225.6 3.9 copy-start
  1229.5 19.5 %copy-start.6 = (f32[1024]{0:T(1024)S(1)}, f32[1024]{0:T(1024)}, u32[]{:S(2)}) copy-start(f32[1024]{0:T(1024)} %param.25) | copy-start | bytes 12292
Sparse Core Ops, SparseCore 0:
  11.3 81.0 all-gather.8
  95.7 76.7 all-gather.4
  175.7 76.7 all-gather.6
  816.4 169.7 all-reduce.3
  988.8 75.1 all-gather.10
  1068.2 152.7 reduce-scatter.7
  1225.7 23.2 reduce-scatter.5
where the time goes:
time: 1260 us
  waiting for transfers between devices  630 us (50%)
  blocking collectives  245 us (19%)
  local copies, waits for them, and re-layouts  171 us (14%)
  matrix products  74.4 us (6%)
  loops' own time  63.8 us (5%)
  other arithmetic  58.4 us (5%)
  between operations  15 us (1%)
    unnamed x9, waiting for transfers between devices  316 us
    pmax x1, blocking collectives, per_device(): peaks = lax.pmax(peaks.astype(jnp.bfloat16), 'pages').astype(peaks.dtype)  245 us
    all_gather x1, waiting for transfers between devices, per_device(): lax.all_gather(rotated_k, 'pages', axis=0, tiled=True)  78.4 us
    all_gather x1, waiting for transfers between devices, per_device(): lax.all_gather(out_weight, 'pages', axis=1, tiled=True)  77 us
    all_gather x1, waiting for transfers between devices, per_device(): lax.all_gather(values, 'pages', axis=0, tiled=True)  73.7 us
    all_gather x1, waiting for transfers between devices, per_device(): lax.all_gather(rotated_q, 'pages', axis=0, tiled=True)  67.2 us
    another operation x2, loops' own time, over_slots(): return lax.fori_loop(0, slot_count, step, start)  63.8 us
    dot_general x24, matrix products, slot_scores(): jnp.einsum('qhd,khd->hqk', query_block, key_block, preferred_element_type...  50.4 us
  transfers between devices with their start and end apart: 7, of which 7 were waited for; matrix products, arithmetic and copies ran while one was open for 3% of the time, Pallas kernels for 0%

commit v1 on v0

--- a/solution.py
+++ b/solution.py
@@ -55,10 +55,16 @@
     positions = (starts + token_ids % span_len).astype(jnp.float32)
     rotated_q = rotate(queries.astype(jnp.float32), positions).astype(jnp.bfloat16)
     rotated_k = rotate(keys.astype(jnp.float32), positions).astype(jnp.bfloat16)
+    ranges_set = lambda here_x: jnp.concatenate(
+        lax.all_to_all(
+            jnp.stack([here_x for _ in range(lax.axis_size("pages"))], axis=0), "pages", 0, 0
+        ),
+        axis=0,
+    )
     all_q, all_k, all_v = (
         lax.all_gather(rotated_q, "pages", axis=0, tiled=True),
         lax.all_gather(rotated_k, "pages", axis=0, tiled=True),
-        lax.all_gather(values, "pages", axis=0, tiled=True),
+        ranges_set(values),
     )
     my_slots = device_at * slot_count + jnp.arange(slot_count, dtype=jnp.int32)
     cached_hit = page_table.reshape(-1)[None, :] == my_slots[:, None]

time: 1260 us -> 1210 us (0.960)
  waiting for transfers between devices: 630 us -> 566 us
    all_gather x1 -> x0, waiting for transfers between devices: 73.7 us -> none  [per_device(): lax.all_gather(values, 'pages', axis=0, tiled=True)]
    all_gather x1, waiting for transfers between devices: 67.2 us -> 41.4 us  [per_device(): lax.all_gather(rotated_q, 'pages', axis=0, tiled=True)]
    all_to_all x0 -> x1, waiting for transfers between devices: none -> 25.1 us  [per_device(): lax.all_to_all(jnp.stack([here_x for _ in range(lax.axis_size('pages'))],...]
    unnamed x9 -> x8, waiting for transfers between devices: 316 us -> 317 us
where the time goes in v1:
time: 1210 us
  waiting for transfers between devices  566 us (47%)
  blocking collectives  245 us (20%)
  local copies, waits for them, and re-layouts  173 us (14%)
  matrix products  74.4 us (6%)
  loops' own time  63.8 us (5%)
  other arithmetic  57.7 us (5%)
  between operations  15 us (1%)
  starting transfers between devices  12.7 us (1%)
    unnamed x8, waiting for transfers between devices  317 us
    pmax x1, blocking collectives, per_device(): peaks = lax.pmax(peaks.astype(jnp.bfloat16), 'pages').astype(peaks.dtype)  245 us
    all_gather x1, waiting for transfers between devices, per_device(): lax.all_gather(rotated_k, 'pages', axis=0, tiled=True)  88.4 us
    all_gather x1, waiting for transfers between devices, per_device(): lax.all_gather(out_weight, 'pages', axis=1, tiled=True)  77 us
    another operation x2, loops' own time, over_slots(): return lax.fori_loop(0, slot_count, step, start)  63.8 us
    dot_general x24, matrix products, slot_scores(): jnp.einsum('qhd,khd->hqk', query_block, key_block, preferred_element_type...  50.4 us
    all_gather x1, waiting for transfers between devices, per_device(): lax.all_gather(rotated_q, 'pages', axis=0, tiled=True)  41.4 us
    and x24, other arithmetic, slot_scores(): cached_ok = is_cached[slot] & (base_pos < length)  29.8 us
  transfers between devices with their start and end apart: 7, of which 7 were waited for; matrix products, arithmetic and copies ran while one was open for 3% of the time, Pallas kernels for 0%

profile of v1, /device:TPU:8, one launch (start us, length us, event | category | flops | bytes accessed | tf_op | source)
XLA Modules:
  0.0 1207.1 jit_solution(7107225212033287395)
XLA Ops:
  11.2 2.7 stack.2
  13.9 12.4 %all-to-all-start = ((bf16[64,72,4,128]{3,1,2,0:T(8,128)(2,1)}), bf16[64,72,4,128]{3,1,2,0:T(8,128)(2,1)}, u32[]{:S(2)}, u32[]{:S(2)}) async-start(bf16[64,72,4,128]{3,1,2,0:T(8,128)(2,1)} %stack.2), calls=%async_computation | async-start | bytes 9437184 | tf_op jit(solution)/shard_map/all_to_all | solution.py:59
  28.4 88.4 %all-gather.6.cloned.1.call-done = bf16[4608,4,128]{2,0,1:T(8,128)(2,1)} async-done(((bf16[72,4,128]{2,0,1:T(8,128)(2,1)}), bf16[4608,4,128]{2,0,1:T(8,128)(2,1)}) %all-gather.6.cloned.1.call-update) | async-done | bytes 4718608 | tf_op jit(solution)/shard_map/all_gather | solution.py:66
  116.8 6.3 copy.79
  123.2 25.1 %all-to-all-done = bf16[64,72,4,128]{3,1,2,0:T(8,128)(2,1)} async-done(((bf16[64,72,4,128]{3,1,2,0:T(8,128)(2,1)}), bf16[64,72,4,128]{3,1,2,0:T(8,128)(2,1)}, u32[]{:S(2)}, u32[]{:S(2)}) %all-to-all-start) | async-done | bytes 4718624 | tf_op jit(solution)/shard_map/all_to_all | solution.py:59
  148.3 3.2 copy.72
  151.5 3.1 copy.73
  154.6 3.2 gather_fusion.1
  157.8 3.2 gather_fusion
  161.0 41.4 %all-gather.4.cloned.1.call-done = bf16[4608,4,128]{2,0,1:T(8,128)(2,1)} async-done(((bf16[72,4,128]{2,0,1:T(8,128)(2,1)}), bf16[4608,4,128]{2,0,1:T(8,128)(2,1)}) %all-gather.4.cloned.1.call-update) | async-done | bytes 4718608 | tf_op jit(solution)/shard_map/all_gather | solution.py:65
  202.4 5.2 copy.83
  209.9 110.6 %while.30 = (s32[]{:T(128)}, bf16[6,768,4]{1,2,0:T(4,128)(2,1)S(1)}, s32[12]{0:T(128)S(1)}, pred[12]{0:T(512)(128)(4,1)S(1)}, s32[12]{0:T(128)S(1)}, /*index=5*/...) while((s32[]{:T(128)}, ...), condition=%wide.region_8.10_spmd.clone, body=%wide.region_6.9_spmd.clone.sunk | while | flops 102147592 | bytes 1153013 | solution.py:117
  320.5 245.0 %pmax.7 = bf16[6,768,4]{1,2,0:T(4,128)(2,1)S(1)} all-reduce(bf16[6,768,4]{1,2,0:T(4,128)(2,1)S(1)} %get-tuple-element.418), channel_id=1, replica_groups=mesh['heads'=4,'pages'=64] {'pages'}, use_global_device_ids=true, to_apply=%region_9.11 | all-reduce | flops 18432 | bytes 73728 | tf_op jit(solution)/shard_map/pmax | solution.py:128
  565.6 4.8 broadcast_in_dim.197.clone
  570.4 194.8 %while.31 = (s32[]{:T(128)}, f32[6,768,4,128]{3,2,1,0:T(4,128)}, f32[6,768,4]{1,2,0:T(4,128)S(1)}, s32[12]{0:T(128)S(1)}, bf16[12,128,4,128]{3,1,2,0:T(8,128)(2,...) while((s32[]{:T(128)}, f32[6,768,4,128]{3,2,1,0:T(4,128)}, ...), condition=%wide.region_12.14_spmd.clone, body=%wide.region_10.13_spmd.clone.sunk | while | flops 203981312 | bytes 18659864 | solution.py:117
  578.1 2.6 fusion.53
  594.3 2.6 fusion.53
  610.5 2.6 fusion.53
  626.8 2.6 fusion.53
  659.2 2.6 fusion.53
  675.5 2.6 fusion.53
  707.9 2.6 fusion.53
  724.1 2.6 fusion.53
  740.4 2.6 fusion.53
  756.7 2.6 fusion.53
  766.5 8.4 copy.107
  776.8 159.0 %all-reduce.4.cloned.1.call-done = f32[4608,4]{0,1:T(4,128)} async-done(((f32[4608,4]{0,1:T(4,128)}), f32[4608,4]{0,1:T(4,128)}) %all-reduce.4.cloned.1.call-update) | async-done | bytes 73744
  936.7 77.0 %all-gather.8.cloned.1.call-done = bf16[512,4096]{0,1:T(8,128)(2,1)} async-done(((bf16[512,64]{0,1:T(8,128)(2,1)}), bf16[512,4096]{0,1:T(8,128)(2,1)}) %all-gather.8.cloned.1.call-update) | async-done | bytes 4194320 | tf_op jit(solution)/shard_map/all_gather | solution.py:175
  1013.7 156.9 %reduce-scatter.8.cloned.1.call-done = f32[72,512]{1,0:T(8,128)} async-done(((f32[4608,512]{1,0:T(8,128)}), f32[72,512]{1,0:T(8,128)}) %reduce-scatter.8.cloned.1.call-update) | async-done | bytes 147472
  1170.8 4.5 convolution_convert_fusion
  1175.3 3.9 copy.87
  1181.5 17.2 %reduce-scatter.6.cloned.1.call-done = bf16[72,1024]{1,0:T(8,128)(2,1)} async-done(((bf16[72,4096]{1,0:T(8,128)(2,1)}), bf16[72,1024]{1,0:T(8,128)(2,1)}) %reduce-scatter.6.cloned.1.call-update) | async-done | bytes 147472 | tf_op jit(solution)/shard_map/reduce_scatter | solution.py:178
  (395 shorter events, 231.0 us)
Async XLA Ops:
  7.2 4.0 copy-start.5
  7.2 109.7 %all-gather.6.cloned.1.call-start = ((), (), s32[]{:S(2)}) async-start(), calls=%async_computation.4 | async-start | bytes 4792320 | tf_op jit(solution)/shard_map/all_gather | solution.py:66
  13.9 12.5 %copy-start.4 = (bf16[72,4,128]{2,1,0:T(4,128)(2,1)S(1)}, bf16[72,4,128]{2,1,0:T(4,128)(2,1)}, u32[]{:S(2)}) copy-start(bf16[72,4,128]{2,1,0:T(4,128)(2,1)} %param.16) | copy-start | bytes 221188
  13.9 13.4 %copy-start.7 = (s32[6,6]{1,0:T(8,128)S(1)}, s32[6,6]{1,0:T(8,128)}, u32[]{:S(2)}) copy-start(s32[6,6]{1,0:T(8,128)} %param.23) | copy-start | bytes 436
  13.9 13.5 %copy-start.8 = (s32[6,122]{1,0:T(8,128)S(1)}, s32[6,122]{1,0:T(8,128)}, u32[]{:S(2)}) copy-start(s32[6,122]{1,0:T(8,128)} %param.22) | copy-start | bytes 8788
  13.9 14.2 %copy-start.9 = (s32[6]{0:T(128)S(1)}, s32[6]{0:T(128)}, u32[]{:S(2)}) copy-start(s32[6]{0:T(128)} %param.21) | copy-start | bytes 76
  13.9 134.4 %all-to-all-start = ((bf16[64,72,4,128]{3,1,2,0:T(8,128)(2,1)}), bf16[64,72,4,128]{3,1,2,0:T(8,128)(2,1)}, u32[]{:S(2)}, u32[]{:S(2)}) async-start(bf16[64,72,4,128]{3,1,2,0:T(8,128)(2,1)} %stack.2), calls=%async_computation | async-start | bytes 9437184 | tf_op jit(solution)/shard_map/all_to_all | solution.py:59
  26.3 176.1 %all-gather.4.cloned.1.call-start = ((), (), s32[]{:S(2)}) async-start(), calls=%async_computation.3 | async-start | bytes 4792320 | tf_op jit(solution)/shard_map/all_gather | solution.py:65
  27.3 908.5 %all-reduce.4.cloned.1.call-start = ((), (), s32[]{:S(2)}) async-start(), calls=%async_computation.7 | async-start | bytes 147456
  202.4 5.2 copy-start.1
  202.4 5.2 copy-start.2
  765.2 0.6 copy-start.3
  765.9 247.8 %all-gather.8.cloned.1.call-start = ((), (), s32[]{:S(2)}) async-start(), calls=%async_computation.5 | async-start | bytes 4259840 | tf_op jit(solution)/shard_map/all_gather | solution.py:175
  766.4 404.2 %reduce-scatter.8.cloned.1.call-start = ((), (), s32[]{:S(2)}) async-start(), calls=%async_computation.8 | async-start | bytes 9584640
  774.9 0.7 copy-start.10
  774.9 423.8 %reduce-scatter.6.cloned.1.call-start = ((), (), s32[]{:S(2)}) async-start(), calls=%async_computation.6 | async-start | bytes 737280 | tf_op jit(solution)/shard_map/reduce_scatter | solution.py:178
  1175.3 3.9 copy-start
  1179.2 19.5 %copy-start.6 = (f32[1024]{0:T(1024)S(1)}, f32[1024]{0:T(1024)}, u32[]{:S(2)}) copy-start(f32[1024]{0:T(1024)} %param.25) | copy-start | bytes 12292
Sparse Core Ops, SparseCore 0:
  11.3 105.5 all-gather.5
  120.1 82.2 all-gather.3
  766.0 169.7 all-reduce.3
  938.4 75.1 all-gather.7
  1017.8 152.7 reduce-scatter.7
  1175.4 23.2 reduce-scatter.5
